TPU v7x, 32 devices: a whole 2x2x4 slice. The times are simulated.
32 devices in a mesh: gx: 8 (over y, x, core), gy: 4 (over z).
Axes of the slice: x: 2, y: 2, z: 4, core: 2. Of those that a mesh axis runs over, the one named last changes fastest.
Arguments:
- particle_count: int32 [8, 256, 1024], P(None, ('gx', 'gy')), may hold values from 0 to 12
- drag_coeff: float32 [8, 256, 1024], P(None, ('gx', 'gy')), may hold values from 0.05 to 2
- particle_velocity: float32 [3, 8, 256, 1024], P(None, None, ('gx', 'gy')), may hold values from -6 to 6
- fluid_velocity: float32 [3, 8, 256, 1024], P(None, None, 'gy', 'gx'), may hold values from -6 to 6
Outputs:
- pressure: float32 [8, 256, 1024], P(None, 'gy', 'gx')
- new_velocity: float32 [3, 8, 256, 1024], P(None, None, ('gx', 'gy'))
- pressure_gradient: float32 [3, 8, 256, 1024], P(None, None, ('gx', 'gy'))
All inputs are finite; a program needn't handle non-finite values.
Results may differ from a plain program's by a relative error of at most 0.00002.
Values sent between devices are 32-bit elements; how exact they have to be, the bound alone decides.
A program may use at most 64 MiB of HBM per device.

v0:
```python
import jax
import jax.numpy as jnp
from jax import lax
from jax.sharding import PartitionSpec as P

SWEEPS = 8
particle_volume = 0.05
time_step = 0.5
viscosity = 0.1


def padded_2(cells, sides, width):
    for axis, dim in sides:
        count = lax.axis_size(axis)
        ends = count - 1
        head = lax.slice_in_dim(cells, 0, width, axis=dim)
        tail = lax.slice_in_dim(cells, cells.shape[dim] - width, cells.shape[dim], axis=dim)
        cells = jnp.concatenate(
            [
                lax.ppermute(tail, axis, [(i, (i + 1) % count) for i in range(ends)]),
                cells,
                lax.ppermute(head, axis, [((i + 1) % count, i) for i in range(ends)]),
            ],
            axis=dim,
        )
    return cells


def pad_depth(values):
    widths = [(0, 0)] * (values.ndim - 3) + [(1, 1), (0, 0), (0, 0)]
    return jnp.pad(values, widths)


def pad_plane(values):
    widths = [(0, 0)] * (values.ndim - 2) + [(1, 1), (1, 1)]
    return jnp.pad(values, widths)


def pad_second(values):
    widths = [(0, 0)] * (values.ndim - 1) + [(1, 1)]
    return jnp.pad(values, widths)


def middle(values):
    return values[..., 1:-1, 1:-1, 1:-1]


def neighbour(values, which):
    if which == 0:
        return values[..., 2:, 1:-1, 1:-1]
    if which == 1:
        return values[..., :-2, 1:-1, 1:-1]
    if which == 2:
        return values[..., 1:-1, 2:, 1:-1]
    if which == 3:
        return values[..., 1:-1, :-2, 1:-1]
    if which == 4:
        return values[..., 1:-1, 1:-1, 2:]
    return values[..., 1:-1, 1:-1, :-2]


def face_weights(voids_wide):
    padded = pad_depth(voids_wide)
    centre = middle(padded)
    weights = jnp.stack([0.5 * (centre + neighbour(padded, which)) for which in range(6)])
    weight_sum = weights[0]
    for which in range(1, 6):
        weight_sum = weight_sum + weights[which]
    return (weights, weight_sum)


def momentum(velocity_wide, weights, voids, drag, drag_force):
    padded = pad_depth(velocity_wide)
    centre = middle(padded)
    diffusion = jnp.zeros_like(centre)
    for which in range(6):
        diffusion = diffusion + weights[which][None] * (neighbour(padded, which) - centre)
    return (voids[None] * centre + time_step * viscosity * diffusion + time_step * drag_force) / (
        voids[None] + time_step * drag[None]
    )


def divergence(flux_wide):
    first = flux_wide[0][:, 2:, 1:-1] - flux_wide[0][:, :-2, 1:-1]
    second = flux_wide[1][:, 1:-1, 2:] - flux_wide[1][:, 1:-1, :-2]
    normal = pad_depth(flux_wide[2])[:, 1:-1, 1:-1]
    third = normal[2:] - normal[:-2]
    return 0.5 * (first + second + third) / time_step


def jacobi_sweep(pressure_wide, weights, weight_sum, source):
    padded = pad_depth(pressure_wide)
    total = weights[0] * neighbour(padded, 0)
    for which in range(1, 6):
        total = total + weights[which] * neighbour(padded, which)
    return (total - source) / weight_sum


def gradient_of(pressure_wide):
    padded = pad_depth(pressure_wide)
    first = 0.5 * (padded[1:-1, 2:, 1:-1] - padded[1:-1, :-2, 1:-1])
    second = 0.5 * (padded[1:-1, 1:-1, 2:] - padded[1:-1, 1:-1, :-2])
    third = 0.5 * (padded[2:, 1:-1, 1:-1] - padded[:-2, 1:-1, 1:-1])
    return jnp.stack([first, second, third])


def order_inward(values, across, along):
    fields, planes, x_rows, y_cols = values.shape
    groups = across // along
    rows_each = x_rows // across
    shaped = values.reshape(fields, planes, along, groups, rows_each, y_cols)
    return jnp.swapaxes(shaped, 2, 3).reshape(fields, planes, x_rows, y_cols)


def order_outward(values, across, along):
    fields, planes, x_rows, y_cols = values.shape
    groups = across // along
    rows_each = x_rows // across
    shaped = values.reshape(fields, planes, groups, along, rows_each, y_cols)
    return jnp.swapaxes(shaped, 2, 3).reshape(fields, planes, x_rows, y_cols)


def to_fluid(fields):
    moved = lax.all_to_all(
        lax.all_to_all(fields, "gx", split_axis=3, concat_axis=2, tiled=True),
        "gy",
        split_axis=2,
        concat_axis=2,
        tiled=True,
    )
    return order_inward(moved, lax.axis_size("gx"), lax.axis_size("gy"))


def to_particles(fields):
    ordered = order_outward(fields, lax.axis_size("gx"), lax.axis_size("gy"))
    return lax.all_to_all(
        lax.all_to_all(ordered, "gy", split_axis=2, concat_axis=2, tiled=True),
        "gx",
        split_axis=2,
        concat_axis=3,
        tiled=True,
    )


def shards(particle_count, drag_coeff, particle_velocity, fluid_velocity):
    voids = 1.0 - particle_count.astype(jnp.float32) * particle_volume
    drag_force = drag_coeff[None] * particle_velocity
    slab_velocity = to_particles(fluid_velocity)
    stacked = jnp.concatenate([slab_velocity, voids[None]], axis=0)
    widened = pad_second(padded_2(stacked, ((("gx", "gy"), 2),), 1))
    weights, weight_sum = face_weights(widened[3])
    predicted = momentum(widened[:3], weights, voids, drag_coeff, drag_force)
    flux = voids[None] * predicted
    flux_first = pad_second(padded_2(flux[0:1], ((("gx", "gy"), 2),), 1))
    flux_wide = jnp.concatenate([flux_first, pad_plane(flux[1:3])], axis=0)
    source = divergence(flux_wide)
    pressure = -source / weight_sum
    for sweep_index in range(SWEEPS - 1):
        pressure_wide = pad_second(padded_2(pressure, ((("gx", "gy"), 1),), 1))
        pressure = jacobi_sweep(pressure_wide, weights, weight_sum, source)
    final_wide = pad_second(padded_2(pressure, ((("gx", "gy"), 1),), 1))
    slopes = gradient_of(final_wide)
    velocity = predicted - time_step * slopes
    pressure_out = to_fluid(pressure[None])[0]
    return (pressure_out, velocity, slopes)


def solution(mesh):
    placed = (
        P(None, ("gx", "gy"), None),
        P(None, ("gx", "gy"), None),
        P(None, None, ("gx", "gy"), None),
        P(None, None, "gy", "gx"),
    )
    return jax.shard_map(
        shards,
        mesh=mesh,
        in_specs=placed,
        out_specs=(
            P(None, "gy", "gx"),
            P(None, None, ("gx", "gy"), None),
            P(None, None, ("gx", "gy"), None),
        ),
        check_vma=False,
    )
```

profile of v0, /device:TPU:0, one launch (start us, length us, event | category | flops | bytes accessed | tf_op | source)
XLA Modules:
  0.0 200.9 jit_solution(16246067221753685963)
XLA Ops:
  2.3 26.5 %all_to_all.46 = f32[3,8,64,128]{3,1,0,2:T(8,128)} all-to-all(f32[3,8,64,128]{3,1,0,2:T(8,128)S(1)} %copy.52), channel_id=1, replica_groups=mesh['gx'=8,'gy'=4] {'gy'}, dimensions={2} | all-to-all | bytes 1572864 | tf_op jit(solution)/shard_map/all_to_all | solution.py:137
  28.8 3.7 %all-to-all-start.1 = ((f32[3,8,64,128]{3,1,0,2:T(8,128)}), f32[3,8,64,128]{3,1,0,2:T(8,128)S(1)}, u32[]{:S(2)}, u32[]{:S(2)}) async-start(f32[3,8,64,128]{3,1,0,2:T(8,128)} %all_to_all.46), calls=%async_computation.1 | async-start | bytes 1572864 | tf_op jit(solution)/shard_map/all_to_all | solution.py:136
  32.9 12.2 %all-to-all-done.1 = f32[3,8,64,128]{3,1,0,2:T(8,128)S(1)} async-done(((f32[3,8,64,128]{3,1,0,2:T(8,128)}), f32[3,8,64,128]{3,1,0,2:T(8,128)S(1)}, u32[]{:S(2)}, u32[]{:S(2)}) %all-to-all-start.1) | async-done | bytes 786464 | tf_op jit(solution)/shard_map/all_to_all | solution.py:136
  45.2 2.1 %collective-permute-start = (f32[4,8,1,1024]{3,1,2,0:T(8,128)S(1)}, f32[4,8,1,1024]{3,1,2,0:T(8,128)S(1)}, u32[]{:S(2)}, u32[]{:S(2)}) collective-permute-start(f32[4,8,1,1024]{3,1,2,0:T(8,128)S(1)} %get-tuple-element.16), channel_id=1, source_target_pairs={{0,1},{1,2},{2,3},{3,4},{4,5},{5,6},{6,7},{7,8},{8,9},{9,10},{10,1... | collective-permute-start | bytes 393224 | tf_op jit(solution)/shard_map/ppermute | solution.py:20
  49.8 4.8 %collective-permute-done.1 = f32[4,8,1,1024]{3,1,2,0:T(8,128)S(1)} collective-permute-done((f32[4,8,1,1024]{3,1,2,0:T(8,128)S(1)}, f32[4,8,1,1024]{3,1,2,0:T(8,128)S(1)}, u32[]{:S(2)}, u32[]{:S(2)}) %collective-permute-start.1) | collective-permute-done | bytes 131104 | tf_op jit(solution)/shard_map/ppermute | solution.py:22
  56.4 1.4 broadcast_multiply_fusion
  57.8 2.5 %collective-permute-start.2 = (f32[1,8,1,1024]{3,1,2,0:T(8,128)S(1)}, f32[1,8,1,1024]{3,1,2,0:T(8,128)S(1)}, u32[]{:S(2)}, u32[]{:S(2)}) collective-permute-start(f32[1,8,1,1024]{3,1,2,0:T(8,128)S(1)} %get-tuple-element.20), channel_id=1, source_target_pairs={{0,1},{1,2},{2,3},{3,4},{4,5},{5,6},{6,7},{7,8},{8,9},{9,10},{10,1... | collective-permute-start | bytes 98312 | tf_op jit(solution)/shard_map/ppermute | solution.py:20
  61.9 4.7 %collective-permute-done.3 = f32[1,8,1,1024]{3,1,2,0:T(8,128)S(1)} collective-permute-done((f32[1,8,1,1024]{3,1,2,0:T(8,128)S(1)}, f32[1,8,1,1024]{3,1,2,0:T(8,128)S(1)}, u32[]{:S(2)}, u32[]{:S(2)}) %collective-permute-start.3) | collective-permute-done | bytes 32800 | tf_op jit(solution)/shard_map/ppermute | solution.py:22
  67.2 3.9 %collective-permute-start.4 = (f32[8,1,1024]{2,0,1:T(8,128)S(1)}, f32[8,1,1024]{2,0,1:T(8,128)S(1)}, u32[]{:S(2)}, u32[]{:S(2)}) collective-permute-start(f32[8,1,1024]{2,0,1:T(8,128)S(1)} %get-tuple-element.46), channel_id=1, source_target_pairs={{0,1},{1,2},{2,3},{3,4},{4,5},{5,6},{6,7},{7,8},{8,9},{9,10},{10,1... | collective-permute-start | bytes 98312 | tf_op jit(solution)/shard_map/ppermute | solution.py:20
  72.7 4.2 %collective-permute-done.5 = f32[8,1,1024]{2,0,1:T(8,128)S(1)} collective-permute-done((f32[8,1,1024]{2,0,1:T(8,128)S(1)}, f32[8,1,1024]{2,0,1:T(8,128)S(1)}, u32[]{:S(2)}, u32[]{:S(2)}) %collective-permute-start.5) | collective-permute-done | bytes 32800 | tf_op jit(solution)/shard_map/ppermute | solution.py:22
  77.6 2.2 %collective-permute-start.6 = (f32[8,1,1024]{2,0,1:T(8,128)S(1)}, f32[8,1,1024]{2,0,1:T(8,128)S(1)}, u32[]{:S(2)}, u32[]{:S(2)}) collective-permute-start(f32[8,1,1024]{2,0,1:T(8,128)S(1)} %get-tuple-element.44), channel_id=1, source_target_pairs={{0,1},{1,2},{2,3},{3,4},{4,5},{5,6},{6,7},{7,8},{8,9},{9,10},{10,1... | collective-permute-start | bytes 98312 | tf_op jit(solution)/shard_map/ppermute | solution.py:20
  81.4 4.2 %collective-permute-done.7 = f32[8,1,1024]{2,0,1:T(8,128)S(1)} collective-permute-done((f32[8,1,1024]{2,0,1:T(8,128)S(1)}, f32[8,1,1024]{2,0,1:T(8,128)S(1)}, u32[]{:S(2)}, u32[]{:S(2)}) %collective-permute-start.7) | collective-permute-done | bytes 32800 | tf_op jit(solution)/shard_map/ppermute | solution.py:22
  86.3 2.9 %collective-permute-start.8 = (f32[8,1,1024]{2,0,1:T(8,128)S(1)}, f32[8,1,1024]{2,0,1:T(8,128)S(1)}, u32[]{:S(2)}, u32[]{:S(2)}) collective-permute-start(f32[8,1,1024]{2,0,1:T(8,128)S(1)} %get-tuple-element.42), channel_id=1, source_target_pairs={{0,1},{1,2},{2,3},{3,4},{4,5},{5,6},{6,7},{7,8},{8,9},{9,10},{10,1... | collective-permute-start | bytes 98312 | tf_op jit(solution)/shard_map/ppermute | solution.py:20
  90.8 4.2 %collective-permute-done.9 = f32[8,1,1024]{2,0,1:T(8,128)S(1)} collective-permute-done((f32[8,1,1024]{2,0,1:T(8,128)S(1)}, f32[8,1,1024]{2,0,1:T(8,128)S(1)}, u32[]{:S(2)}, u32[]{:S(2)}) %collective-permute-start.9) | collective-permute-done | bytes 32800 | tf_op jit(solution)/shard_map/ppermute | solution.py:22
  95.6 4.1 %collective-permute-start.10 = (f32[8,1,1024]{2,0,1:T(8,128)S(1)}, f32[8,1,1024]{2,0,1:T(8,128)S(1)}, u32[]{:S(2)}, u32[]{:S(2)}) collective-permute-start(f32[8,1,1024]{2,0,1:T(8,128)S(1)} %get-tuple-element.40), channel_id=1, source_target_pairs={{0,1},{1,2},{2,3},{3,4},{4,5},{5,6},{6,7},{7,8},{8,9},{9,10},{10,1... | collective-permute-start | bytes 98312 | tf_op jit(solution)/shard_map/ppermute | solution.py:20
  101.3 4.6 %collective-permute-done.11 = f32[8,1,1024]{2,0,1:T(8,128)S(1)} collective-permute-done((f32[8,1,1024]{2,0,1:T(8,128)S(1)}, f32[8,1,1024]{2,0,1:T(8,128)S(1)}, u32[]{:S(2)}, u32[]{:S(2)}) %collective-permute-start.11) | collective-permute-done | bytes 32800 | tf_op jit(solution)/shard_map/ppermute | solution.py:22
  106.5 3.9 %collective-permute-start.12 = (f32[8,1,1024]{2,0,1:T(8,128)S(1)}, f32[8,1,1024]{2,0,1:T(8,128)S(1)}, u32[]{:S(2)}, u32[]{:S(2)}) collective-permute-start(f32[8,1,1024]{2,0,1:T(8,128)S(1)} %get-tuple-element.38), channel_id=1, source_target_pairs={{0,1},{1,2},{2,3},{3,4},{4,5},{5,6},{6,7},{7,8},{8,9},{9,10},{10,1... | collective-permute-start | bytes 98312 | tf_op jit(solution)/shard_map/ppermute | solution.py:20
  112.1 4.6 %collective-permute-done.13 = f32[8,1,1024]{2,0,1:T(8,128)S(1)} collective-permute-done((f32[8,1,1024]{2,0,1:T(8,128)S(1)}, f32[8,1,1024]{2,0,1:T(8,128)S(1)}, u32[]{:S(2)}, u32[]{:S(2)}) %collective-permute-start.13) | collective-permute-done | bytes 32800 | tf_op jit(solution)/shard_map/ppermute | solution.py:22
  117.3 3.7 %collective-permute-start.14 = (f32[8,1,1024]{2,0,1:T(8,128)S(1)}, f32[8,1,1024]{2,0,1:T(8,128)S(1)}, u32[]{:S(2)}, u32[]{:S(2)}) collective-permute-start(f32[8,1,1024]{2,0,1:T(8,128)S(1)} %get-tuple-element.36), channel_id=1, source_target_pairs={{0,1},{1,2},{2,3},{3,4},{4,5},{5,6},{6,7},{7,8},{8,9},{9,10},{10,1... | collective-permute-start | bytes 98312 | tf_op jit(solution)/shard_map/ppermute | solution.py:20
  122.6 4.6 %collective-permute-done.15 = f32[8,1,1024]{2,0,1:T(8,128)S(1)} collective-permute-done((f32[8,1,1024]{2,0,1:T(8,128)S(1)}, f32[8,1,1024]{2,0,1:T(8,128)S(1)}, u32[]{:S(2)}, u32[]{:S(2)}) %collective-permute-start.15) | collective-permute-done | bytes 32800 | tf_op jit(solution)/shard_map/ppermute | solution.py:22
  127.7 3.7 %collective-permute-start.16 = (f32[8,1,1024]{2,0,1:T(8,128)S(1)}, f32[8,1,1024]{2,0,1:T(8,128)S(1)}, u32[]{:S(2)}, u32[]{:S(2)}) collective-permute-start(f32[8,1,1024]{2,0,1:T(8,128)S(1)} %get-tuple-element.34), channel_id=1, source_target_pairs={{0,1},{1,2},{2,3},{3,4},{4,5},{5,6},{6,7},{7,8},{8,9},{9,10},{10,1... | collective-permute-start | bytes 98312 | tf_op jit(solution)/shard_map/ppermute | solution.py:20
  133.0 4.6 %collective-permute-done.17 = f32[8,1,1024]{2,0,1:T(8,128)S(1)} collective-permute-done((f32[8,1,1024]{2,0,1:T(8,128)S(1)}, f32[8,1,1024]{2,0,1:T(8,128)S(1)}, u32[]{:S(2)}, u32[]{:S(2)}) %collective-permute-start.17) | collective-permute-done | bytes 32800 | tf_op jit(solution)/shard_map/ppermute | solution.py:22
  139.5 4.5 %collective-permute-start.19 = (f32[8,1,1024]{2,0,1:T(8,128)S(1)}, f32[8,1,1024]{2,0,1:T(8,128)S(1)}, u32[]{:S(2)}, u32[]{:S(2)}) collective-permute-start(f32[8,1,1024]{2,0,1:T(8,128)S(1)} %get-tuple-element.32), channel_id=1, source_target_pairs={{0,1},{1,2},{2,3},{3,4},{4,5},{5,6},{6,7},{7,8},{8,9},{9,10},{10,1... | collective-permute-start | bytes 98312 | tf_op jit(solution)/shard_map/ppermute | solution.py:20
  144.1 2.7 %copy.58 = f32[1,8,8,1024]{2,1,0,3:T(8,128)} copy(f32[1,8,8,1024]{3,1,2,0:T(8,128)S(1)} %bitcast.42) | data formatting | bytes 524288 | tf_op jit(solution)/shard_map/broadcast_in_dim | solution.py:164
  146.8 4.4 %reshape.29 = f32[8,1,8192]{2,1,0:T(1,128)} reshape(f32[1024,1,8,8]{3,2,1,0:T(8,128)} %bitcast.38) | data formatting | bytes 524288
  151.2 18.5 %all-to-all-start.2 = ((f32[8,1,8192]{2,1,0:T(1,128)}), f32[8,1,8192]{2,1,0:T(1,128)S(1)}, u32[]{:S(2)}, u32[]{:S(2)}) async-start(f32[8,1,8192]{2,1,0:T(1,128)} %reshape.29), calls=%async_computation.2 | async-start | bytes 524288 | tf_op jit(solution)/shard_map/all_to_all | solution.py:125
  169.8 6.7 %all-to-all-done.2 = f32[8,1,8192]{2,1,0:T(1,128)S(1)} async-done(((f32[8,1,8192]{2,1,0:T(1,128)}), f32[8,1,8192]{2,1,0:T(1,128)S(1)}, u32[]{:S(2)}, u32[]{:S(2)}) %all-to-all-start.2) | async-done | bytes 262176 | tf_op jit(solution)/shard_map/all_to_all | solution.py:125
  178.4 4.3 %reshape.30 = f32[1024,1,8,8]{3,2,1,0:T(8,128)} reshape(f32[8,8192]{1,0:T(8,128)S(1)} %reduce) | data formatting | bytes 524288
  182.7 3.5 %copy.59 = f32[1,8,8,8,128]{4,1,3,2,0:T(8,128)} copy(f32[1,8,8,8,128]{3,1,4,2,0:T(8,128)} %bitcast.37) | data formatting | bytes 524288 | tf_op jit(solution)/shard_map/all_to_all | solution.py:125
  186.1 5.7 %all-to-all-start.3 = ((f32[1,8,64,128]{3,1,0,2:T(8,128)}), f32[1,8,64,128]{3,1,0,2:T(8,128)S(1)}, u32[]{:S(2)}, u32[]{:S(2)}) async-start(f32[1,8,64,128]{3,1,0,2:T(8,128)} %bitcast.14), calls=%async_computation.3 | async-start | bytes 524288 | tf_op jit(solution)/shard_map/all_to_all | solution.py:124
  192.2 1.3 copy.62
  194.9 5.2 %all-to-all-done.3 = f32[1,8,64,128]{3,1,0,2:T(8,128)S(1)} async-done(((f32[1,8,64,128]{3,1,0,2:T(8,128)}), f32[1,8,64,128]{3,1,0,2:T(8,128)S(1)}, u32[]{:S(2)}, u32[]{:S(2)}) %all-to-all-start.3) | async-done | bytes 262176 | tf_op jit(solution)/shard_map/all_to_all | solution.py:124
  (72 shorter events, 29.5 us)
Async XLA Ops:
  2.3 30.2 %copy-start.1 = (f32[8,8,1024]{2,1,0:T(8,128)S(1)}, f32[8,8,1024]{2,1,0:T(8,128)}, u32[]{:S(2)}) copy-start(f32[8,8,1024]{2,1,0:T(8,128)} %param.5) | copy-start | bytes 786436
  2.3 30.2 %copy-start.2 = (s32[8,8,1024]{2,1,0:T(8,128)S(1)}, s32[8,8,1024]{2,1,0:T(8,128)}, u32[]{:S(2)}) copy-start(s32[8,8,1024]{2,1,0:T(8,128)} %param.4) | copy-start | bytes 786436
  28.8 16.3 %all-to-all-start.1 = ((f32[3,8,64,128]{3,1,0,2:T(8,128)}), f32[3,8,64,128]{3,1,0,2:T(8,128)S(1)}, u32[]{:S(2)}, u32[]{:S(2)}) async-start(f32[3,8,64,128]{3,1,0,2:T(8,128)} %all_to_all.46), calls=%async_computation.1 | async-start | bytes 1572864 | tf_op jit(solution)/shard_map/all_to_all | solution.py:136
  45.2 4.6 %collective-permute-start = (f32[4,8,1,1024]{3,1,2,0:T(8,128)S(1)}, f32[4,8,1,1024]{3,1,2,0:T(8,128)S(1)}, u32[]{:S(2)}, u32[]{:S(2)}) collective-permute-start(f32[4,8,1,1024]{3,1,2,0:T(8,128)S(1)} %get-tuple-element.16), channel_id=1, source_target_pairs={{0,1},{1,2},{2,3},{3,4},{4,5},{5,6},{6,7},{7,8},{8,9},{9,10},{10,1... | collective-permute-start | bytes 393224 | tf_op jit(solution)/shard_map/ppermute | solution.py:20
  47.3 7.3 %collective-permute-start.1 = (f32[4,8,1,1024]{3,1,2,0:T(8,128)S(1)}, f32[4,8,1,1024]{3,1,2,0:T(8,128)S(1)}, u32[]{:S(2)}, u32[]{:S(2)}) collective-permute-start(f32[4,8,1,1024]{3,1,2,0:T(8,128)S(1)} %get-tuple-element.17), channel_id=1, source_target_pairs={{1,0},{2,1},{3,2},{4,3},{5,4},{6,5},{7,6},{8,7},{9,8},{10,9},{11,1... | collective-permute-start | bytes 393224 | tf_op jit(solution)/shard_map/ppermute | solution.py:22
  55.2 1.1 copy-start
  57.8 4.1 %collective-permute-start.2 = (f32[1,8,1,1024]{3,1,2,0:T(8,128)S(1)}, f32[1,8,1,1024]{3,1,2,0:T(8,128)S(1)}, u32[]{:S(2)}, u32[]{:S(2)}) collective-permute-start(f32[1,8,1,1024]{3,1,2,0:T(8,128)S(1)} %get-tuple-element.20), channel_id=1, source_target_pairs={{0,1},{1,2},{2,3},{3,4},{4,5},{5,6},{6,7},{7,8},{8,9},{9,10},{10,1... | collective-permute-start | bytes 98312 | tf_op jit(solution)/shard_map/ppermute | solution.py:20
  60.3 6.3 %collective-permute-start.3 = (f32[1,8,1,1024]{3,1,2,0:T(8,128)S(1)}, f32[1,8,1,1024]{3,1,2,0:T(8,128)S(1)}, u32[]{:S(2)}, u32[]{:S(2)}) collective-permute-start(f32[1,8,1,1024]{3,1,2,0:T(8,128)S(1)} %get-tuple-element.21), channel_id=1, source_target_pairs={{1,0},{2,1},{3,2},{4,3},{5,4},{6,5},{7,6},{8,7},{9,8},{10,9},{11,1... | collective-permute-start | bytes 98312 | tf_op jit(solution)/shard_map/ppermute | solution.py:22
  67.2 5.5 %collective-permute-start.4 = (f32[8,1,1024]{2,0,1:T(8,128)S(1)}, f32[8,1,1024]{2,0,1:T(8,128)S(1)}, u32[]{:S(2)}, u32[]{:S(2)}) collective-permute-start(f32[8,1,1024]{2,0,1:T(8,128)S(1)} %get-tuple-element.46), channel_id=1, source_target_pairs={{0,1},{1,2},{2,3},{3,4},{4,5},{5,6},{6,7},{7,8},{8,9},{9,10},{10,1... | collective-permute-start | bytes 98312 | tf_op jit(solution)/shard_map/ppermute | solution.py:20
  71.2 5.8 %collective-permute-start.5 = (f32[8,1,1024]{2,0,1:T(8,128)S(1)}, f32[8,1,1024]{2,0,1:T(8,128)S(1)}, u32[]{:S(2)}, u32[]{:S(2)}) collective-permute-start(f32[8,1,1024]{2,0,1:T(8,128)S(1)} %get-tuple-element.47), channel_id=1, source_target_pairs={{1,0},{2,1},{3,2},{4,3},{5,4},{6,5},{7,6},{8,7},{9,8},{10,9},{11,1... | collective-permute-start | bytes 98312 | tf_op jit(solution)/shard_map/ppermute | solution.py:22
  77.6 3.8 %collective-permute-start.6 = (f32[8,1,1024]{2,0,1:T(8,128)S(1)}, f32[8,1,1024]{2,0,1:T(8,128)S(1)}, u32[]{:S(2)}, u32[]{:S(2)}) collective-permute-start(f32[8,1,1024]{2,0,1:T(8,128)S(1)} %get-tuple-element.44), channel_id=1, source_target_pairs={{0,1},{1,2},{2,3},{3,4},{4,5},{5,6},{6,7},{7,8},{8,9},{9,10},{10,1... | collective-permute-start | bytes 98312 | tf_op jit(solution)/shard_map/ppermute | solution.py:20
  79.8 5.8 %collective-permute-start.7 = (f32[8,1,1024]{2,0,1:T(8,128)S(1)}, f32[8,1,1024]{2,0,1:T(8,128)S(1)}, u32[]{:S(2)}, u32[]{:S(2)}) collective-permute-start(f32[8,1,1024]{2,0,1:T(8,128)S(1)} %get-tuple-element.45), channel_id=1, source_target_pairs={{1,0},{2,1},{3,2},{4,3},{5,4},{6,5},{7,6},{8,7},{9,8},{10,9},{11,1... | collective-permute-start | bytes 98312 | tf_op jit(solution)/shard_map/ppermute | solution.py:22
  86.3 4.5 %collective-permute-start.8 = (f32[8,1,1024]{2,0,1:T(8,128)S(1)}, f32[8,1,1024]{2,0,1:T(8,128)S(1)}, u32[]{:S(2)}, u32[]{:S(2)}) collective-permute-start(f32[8,1,1024]{2,0,1:T(8,128)S(1)} %get-tuple-element.42), channel_id=1, source_target_pairs={{0,1},{1,2},{2,3},{3,4},{4,5},{5,6},{6,7},{7,8},{8,9},{9,10},{10,1... | collective-permute-start | bytes 98312 | tf_op jit(solution)/shard_map/ppermute | solution.py:20
  89.2 5.8 %collective-permute-start.9 = (f32[8,1,1024]{2,0,1:T(8,128)S(1)}, f32[8,1,1024]{2,0,1:T(8,128)S(1)}, u32[]{:S(2)}, u32[]{:S(2)}) collective-permute-start(f32[8,1,1024]{2,0,1:T(8,128)S(1)} %get-tuple-element.43), channel_id=1, source_target_pairs={{1,0},{2,1},{3,2},{4,3},{5,4},{6,5},{7,6},{8,7},{9,8},{10,9},{11,1... | collective-permute-start | bytes 98312 | tf_op jit(solution)/shard_map/ppermute | solution.py:22
  95.6 5.7 %collective-permute-start.10 = (f32[8,1,1024]{2,0,1:T(8,128)S(1)}, f32[8,1,1024]{2,0,1:T(8,128)S(1)}, u32[]{:S(2)}, u32[]{:S(2)}) collective-permute-start(f32[8,1,1024]{2,0,1:T(8,128)S(1)} %get-tuple-element.40), channel_id=1, source_target_pairs={{0,1},{1,2},{2,3},{3,4},{4,5},{5,6},{6,7},{7,8},{8,9},{9,10},{10,1... | collective-permute-start | bytes 98312 | tf_op jit(solution)/shard_map/ppermute | solution.py:20
  99.7 6.2 %collective-permute-start.11 = (f32[8,1,1024]{2,0,1:T(8,128)S(1)}, f32[8,1,1024]{2,0,1:T(8,128)S(1)}, u32[]{:S(2)}, u32[]{:S(2)}) collective-permute-start(f32[8,1,1024]{2,0,1:T(8,128)S(1)} %get-tuple-element.41), channel_id=1, source_target_pairs={{1,0},{2,1},{3,2},{4,3},{5,4},{6,5},{7,6},{8,7},{9,8},{10,9},{11,1... | collective-permute-start | bytes 98312 | tf_op jit(solution)/shard_map/ppermute | solution.py:22
  106.5 5.5 %collective-permute-start.12 = (f32[8,1,1024]{2,0,1:T(8,128)S(1)}, f32[8,1,1024]{2,0,1:T(8,128)S(1)}, u32[]{:S(2)}, u32[]{:S(2)}) collective-permute-start(f32[8,1,1024]{2,0,1:T(8,128)S(1)} %get-tuple-element.38), channel_id=1, source_target_pairs={{0,1},{1,2},{2,3},{3,4},{4,5},{5,6},{6,7},{7,8},{8,9},{9,10},{10,1... | collective-permute-start | bytes 98312 | tf_op jit(solution)/shard_map/ppermute | solution.py:20
  110.5 6.1 %collective-permute-start.13 = (f32[8,1,1024]{2,0,1:T(8,128)S(1)}, f32[8,1,1024]{2,0,1:T(8,128)S(1)}, u32[]{:S(2)}, u32[]{:S(2)}) collective-permute-start(f32[8,1,1024]{2,0,1:T(8,128)S(1)} %get-tuple-element.39), channel_id=1, source_target_pairs={{1,0},{2,1},{3,2},{4,3},{5,4},{6,5},{7,6},{8,7},{9,8},{10,9},{11,1... | collective-permute-start | bytes 98312 | tf_op jit(solution)/shard_map/ppermute | solution.py:22
  117.3 5.3 %collective-permute-start.14 = (f32[8,1,1024]{2,0,1:T(8,128)S(1)}, f32[8,1,1024]{2,0,1:T(8,128)S(1)}, u32[]{:S(2)}, u32[]{:S(2)}) collective-permute-start(f32[8,1,1024]{2,0,1:T(8,128)S(1)} %get-tuple-element.36), channel_id=1, source_target_pairs={{0,1},{1,2},{2,3},{3,4},{4,5},{5,6},{6,7},{7,8},{8,9},{9,10},{10,1... | collective-permute-start | bytes 98312 | tf_op jit(solution)/shard_map/ppermute | solution.py:20
  121.0 6.1 %collective-permute-start.15 = (f32[8,1,1024]{2,0,1:T(8,128)S(1)}, f32[8,1,1024]{2,0,1:T(8,128)S(1)}, u32[]{:S(2)}, u32[]{:S(2)}) collective-permute-start(f32[8,1,1024]{2,0,1:T(8,128)S(1)} %get-tuple-element.37), channel_id=1, source_target_pairs={{1,0},{2,1},{3,2},{4,3},{5,4},{6,5},{7,6},{8,7},{9,8},{10,9},{11,1... | collective-permute-start | bytes 98312 | tf_op jit(solution)/shard_map/ppermute | solution.py:22
  127.7 5.3 %collective-permute-start.16 = (f32[8,1,1024]{2,0,1:T(8,128)S(1)}, f32[8,1,1024]{2,0,1:T(8,128)S(1)}, u32[]{:S(2)}, u32[]{:S(2)}) collective-permute-start(f32[8,1,1024]{2,0,1:T(8,128)S(1)} %get-tuple-element.34), channel_id=1, source_target_pairs={{0,1},{1,2},{2,3},{3,4},{4,5},{5,6},{6,7},{7,8},{8,9},{9,10},{10,1... | collective-permute-start | bytes 98312 | tf_op jit(solution)/shard_map/ppermute | solution.py:20
  131.5 6.1 %collective-permute-start.17 = (f32[8,1,1024]{2,0,1:T(8,128)S(1)}, f32[8,1,1024]{2,0,1:T(8,128)S(1)}, u32[]{:S(2)}, u32[]{:S(2)}) collective-permute-start(f32[8,1,1024]{2,0,1:T(8,128)S(1)} %get-tuple-element.35), channel_id=1, source_target_pairs={{1,0},{2,1},{3,2},{4,3},{5,4},{6,5},{7,6},{8,7},{9,8},{10,9},{11,1... | collective-permute-start | bytes 98312 | tf_op jit(solution)/shard_map/ppermute | solution.py:22
  138.2 31.4 %collective-permute-start.18 = (f32[8,1,1024]{2,0,1:T(8,128)S(1)}, f32[8,1,1024]{2,0,1:T(8,128)S(1)}, u32[]{:S(2)}, u32[]{:S(2)}) collective-permute-start(f32[8,1,1024]{2,0,1:T(8,128)S(1)} %get-tuple-element.33), channel_id=1, source_target_pairs={{1,0},{2,1},{3,2},{4,3},{5,4},{6,5},{7,6},{8,7},{9,8},{10,9},{11,1... | collective-permute-start | bytes 98312 | tf_op jit(solution)/shard_map/ppermute | solution.py:22
  139.5 30.1 %collective-permute-start.19 = (f32[8,1,1024]{2,0,1:T(8,128)S(1)}, f32[8,1,1024]{2,0,1:T(8,128)S(1)}, u32[]{:S(2)}, u32[]{:S(2)}) collective-permute-start(f32[8,1,1024]{2,0,1:T(8,128)S(1)} %get-tuple-element.32), channel_id=1, source_target_pairs={{0,1},{1,2},{2,3},{3,4},{4,5},{5,6},{6,7},{7,8},{8,9},{9,10},{10,1... | collective-permute-start | bytes 98312 | tf_op jit(solution)/shard_map/ppermute | solution.py:20
  151.2 25.4 %all-to-all-start.2 = ((f32[8,1,8192]{2,1,0:T(1,128)}), f32[8,1,8192]{2,1,0:T(1,128)S(1)}, u32[]{:S(2)}, u32[]{:S(2)}) async-start(f32[8,1,8192]{2,1,0:T(1,128)} %reshape.29), calls=%async_computation.2 | async-start | bytes 524288 | tf_op jit(solution)/shard_map/all_to_all | solution.py:125
  186.1 14.0 %all-to-all-start.3 = ((f32[1,8,64,128]{3,1,0,2:T(8,128)}), f32[1,8,64,128]{3,1,0,2:T(8,128)S(1)}, u32[]{:S(2)}, u32[]{:S(2)}) async-start(f32[1,8,64,128]{3,1,0,2:T(8,128)} %bitcast.14), calls=%async_computation.3 | async-start | bytes 524288 | tf_op jit(solution)/shard_map/all_to_all | solution.py:124
where the time goes:
time: 202 us; the launch traced here: 201 us
  starting transfers between devices  74.5 us (37%)
  waiting for transfers between devices  67.8 us (34%)
  blocking collectives  26.5 us (13%)
  local copies, waits for them, and re-layouts  21.6 us (11%)
  other arithmetic  9.39 us (5%)
    ppermute x10, waiting for transfers between devices, padded_2(): lax.ppermute(head, axis, [((i + 1) % count, i) for i in range(ends)])  40.5 us
    ppermute x10, starting transfers between devices, padded_2(): lax.ppermute(tail, axis, [(i, (i + 1) % count) for i in range(ends)])  33.7 us
    all_to_all x1, blocking collectives, to_particles(): lax.all_to_all(ordered, 'gy', split_axis=2, concat_axis=2, tiled=True)  26.5 us
    all_to_all x1, starting transfers between devices, to_fluid(): lax.all_to_all(fields, 'gx', split_axis=3, concat_axis=2, tiled=True)  18.5 us
    ppermute x10, starting transfers between devices, padded_2(): lax.ppermute(head, axis, [((i + 1) % count, i) for i in range(ends)])  12.9 us
    all_to_all x1, waiting for transfers between devices, to_particles(): lax.all_to_all(lax.all_to_all(ordered, 'gy', split_axis=2, concat_axis=2,...  12.2 us
    unnamed x10, local copies, waits for them, and re-layouts  12.1 us
    all_to_all x1, waiting for transfers between devices, to_fluid(): lax.all_to_all(fields, 'gx', split_axis=3, concat_axis=2, tiled=True)  6.72 us
  transfers between devices with their start and end apart: 23, of which 20 were waited for; matrix products, arithmetic and copies ran while one was open for 5% of the time, Pallas kernels for 0%

commit v1 on v0

--- a/solution.py
+++ b/solution.py
@@ -7,6 +7,29 @@
 particle_volume = 0.05
 time_step = 0.5
 viscosity = 0.1
+
+
+def cut_along(array, dim, length):
+    shape = array.shape
+    blocks = array.reshape(*shape[:dim], length, shape[dim] // length, *shape[dim + 1 :])
+    return jnp.moveaxis(blocks, dim, 0)
+
+
+def joined_along(parts, dim):
+    parts = jnp.moveaxis(parts, 0, dim)
+    lengths = parts.shape
+    return parts.reshape(*lengths[:dim], lengths[dim] * lengths[dim + 1], *lengths[dim + 2 :])
+
+
+def exchange_directly(shard, axis, split_dim, concat_dim):
+    devices, index = (lax.axis_size(axis), lax.axis_index(axis))
+    parts = cut_along(shard, split_dim, devices)
+    done = [parts[index]]
+    for step in range(1, devices):
+        sent = parts[(index + step) % devices]
+        done.append(lax.ppermute(sent, axis, [(i, (i + step) % devices) for i in range(devices)]))
+    parts = jnp.stack(done)[(index - jnp.arange(devices)) % devices]
+    return joined_along(parts, concat_dim)
 
 
 def padded_2(cells, sides, width):
@@ -122,11 +145,7 @@
 
 def to_fluid(fields):
     moved = lax.all_to_all(
-        lax.all_to_all(fields, "gx", split_axis=3, concat_axis=2, tiled=True),
-        "gy",
-        split_axis=2,
-        concat_axis=2,
-        tiled=True,
+        exchange_directly(fields, "gx", 3, 2), "gy", split_axis=2, concat_axis=2, tiled=True
     )
     return order_inward(moved, lax.axis_size("gx"), lax.axis_size("gy"))
 

time: 202 us -> 191 us (0.946)
  local copies, waits for them, and re-layouts: 21.6 us -> 5.81 us
  starting transfers between devices: 74.5 us -> 79.6 us
  waiting for transfers between devices: 67.8 us -> 64.3 us
  other arithmetic: 9.39 us -> 12.1 us
    ppermute x0 -> x7, starting transfers between devices: none -> 25.7 us  [exchange_directly(): lax.ppermute(sent, axis, [(i, (i + step) % devices) for i in range(device...]
    all_to_all x2 -> x1, starting transfers between devices: 24.2 us -> 3.41 us  [to_fluid(): lax.all_to_all(exchange_directly(fields, 'gx', 3, 2), 'gy', split_axis=2,...]
    unnamed x10 -> x13, local copies, waits for them, and re-layouts: 12.1 us -> 0.71 us
    all_to_all x2 -> x1, waiting for transfers between devices: 11.9 us -> 7.13 us  [to_fluid(): lax.all_to_all(exchange_directly(fields, 'gx', 3, 2), 'gy', split_axis=2,...]
    all_to_all x3 -> x1, local copies, waits for them, and re-layouts: 4.02 us -> 0.05 us  [to_fluid(): lax.all_to_all(exchange_directly(fields, 'gx', 3, 2), 'gy', split_axis=2,...]
    concatenate x9, other arithmetic: 1.73 us -> 4.76 us  [padded_2(): jnp.concatenate([lax.ppermute(tail, axis, [(i, (i + 1) % count) for i in...]
    broadcast_in_dim x1 -> x0, local copies, waits for them, and re-layouts: 2.66 us -> none  [shards(): pressure_out = to_fluid(pressure[None])[0]]
  transfers between devices with their start and end apart: 23 -> 29, of which waited for: 20 -> 20; matrix products, arithmetic and copies ran while one was open for 5% -> 1% of each run, Pallas kernels for 0% -> 0%
where the time goes in v1:
time: 191 us; the launch traced here: 189 us
  starting transfers between devices  79.6 us (42%)
  waiting for transfers between devices  64.3 us (34%)
  blocking collectives  26.4 us (14%)
  other arithmetic  12.1 us (6%)
  local copies, waits for them, and re-layouts  5.81 us (3%)
    ppermute x10, waiting for transfers between devices, padded_2(): lax.ppermute(head, axis, [((i + 1) % count, i) for i in range(ends)])  40.3 us
    ppermute x10, starting transfers between devices, padded_2(): lax.ppermute(tail, axis, [(i, (i + 1) % count) for i in range(ends)])  33.7 us
    all_to_all x1, blocking collectives, to_particles(): lax.all_to_all(ordered, 'gy', split_axis=2, concat_axis=2, tiled=True)  26.4 us
    ppermute x7, starting transfers between devices, exchange_directly(): lax.ppermute(sent, axis, [(i, (i + step) % devices) for i in range(device...  25.7 us
    ppermute x10, starting transfers between devices, padded_2(): lax.ppermute(head, axis, [((i + 1) % count, i) for i in range(ends)])  13.1 us
    all_to_all x1, waiting for transfers between devices, to_particles(): lax.all_to_all(lax.all_to_all(ordered, 'gy', split_axis=2, concat_axis=2,...  12.5 us
    all_to_all x1, waiting for transfers between devices, to_fluid(): lax.all_to_all(exchange_directly(fields, 'gx', 3, 2), 'gy', split_axis=2,...  7.13 us
    concatenate x9, other arithmetic, padded_2(): jnp.concatenate([lax.ppermute(tail, axis, [(i, (i + 1) % count) for i in...  4.76 us
  transfers between devices with their start and end apart: 29, of which 20 were waited for; matrix products, arithmetic and copies ran while one was open for 1% of the time, Pallas kernels for 0%

profile of v1, /device:TPU:0, one launch (start us, length us, event | category | flops | bytes accessed | tf_op | source)
XLA Modules:
  0.0 189.4 jit_solution(1856491226234648268)
XLA Ops:
  2.3 26.4 %all_to_all.28 = f32[3,8,64,128]{3,1,0,2:T(8,128)} all-to-all(f32[3,8,64,128]{3,1,0,2:T(8,128)S(1)} %copy.19), channel_id=1, replica_groups=mesh['gx'=8,'gy'=4] {'gy'}, dimensions={2} | all-to-all | bytes 1572864 | tf_op jit(solution)/shard_map/all_to_all | solution.py:156
  28.7 3.7 %all-to-all-start.1 = ((f32[3,8,64,128]{3,1,0,2:T(8,128)}), f32[3,8,64,128]{3,1,0,2:T(8,128)S(1)}, u32[]{:S(2)}, u32[]{:S(2)}) async-start(f32[3,8,64,128]{3,1,0,2:T(8,128)} %all_to_all.28), calls=%async_computation.1 | async-start | bytes 1572864 | tf_op jit(solution)/shard_map/all_to_all | solution.py:155
  32.5 12.5 %all-to-all-done.1 = f32[3,8,64,128]{3,1,0,2:T(8,128)S(1)} async-done(((f32[3,8,64,128]{3,1,0,2:T(8,128)}), f32[3,8,64,128]{3,1,0,2:T(8,128)S(1)}, u32[]{:S(2)}, u32[]{:S(2)}) %all-to-all-start.1) | async-done | bytes 786464 | tf_op jit(solution)/shard_map/all_to_all | solution.py:155
  45.3 2.1 %collective-permute-start = (f32[4,8,1,1024]{3,2,1,0:T(1,128)S(1)}, f32[4,8,1,1024]{3,2,1,0:T(1,128)S(1)}, u32[]{:S(2)}, u32[]{:S(2)}) collective-permute-start(f32[4,8,1,1024]{3,2,1,0:T(1,128)S(1)} %get-tuple-element.9), channel_id=1, source_target_pairs={{0,1},{1,2},{2,3},{3,4},{4,5},{5,6},{6,7},{7,8},{8,9},{9,10},{10,1... | collective-permute-start | bytes 393224 | tf_op jit(solution)/shard_map/ppermute | solution.py:43
  49.9 4.8 %collective-permute-done.1 = f32[4,8,1,1024]{3,2,1,0:T(1,128)S(1)} collective-permute-done((f32[4,8,1,1024]{3,2,1,0:T(1,128)S(1)}, f32[4,8,1,1024]{3,2,1,0:T(1,128)S(1)}, u32[]{:S(2)}, u32[]{:S(2)}) %collective-permute-start.1) | collective-permute-done | bytes 131104 | tf_op jit(solution)/shard_map/ppermute | solution.py:45
  54.7 1.4 select_maximum_fusion
  58.9 2.5 %collective-permute-start.2 = (f32[1,8,1,1024]{3,2,1,0:T(1,128)S(1)}, f32[1,8,1,1024]{3,2,1,0:T(1,128)S(1)}, u32[]{:S(2)}, u32[]{:S(2)}) collective-permute-start(f32[1,8,1,1024]{3,2,1,0:T(1,128)S(1)} %get-tuple-element.11), channel_id=1, source_target_pairs={{0,1},{1,2},{2,3},{3,4},{4,5},{5,6},{6,7},{7,8},{8,9},{9,10},{10,1... | collective-permute-start | bytes 98312 | tf_op jit(solution)/shard_map/ppermute | solution.py:43
  63.1 4.5 %collective-permute-done.3 = f32[1,8,1,1024]{3,2,1,0:T(1,128)S(1)} collective-permute-done((f32[1,8,1,1024]{3,2,1,0:T(1,128)S(1)}, f32[1,8,1,1024]{3,2,1,0:T(1,128)S(1)}, u32[]{:S(2)}, u32[]{:S(2)}) %collective-permute-start.3) | collective-permute-done | bytes 32800 | tf_op jit(solution)/shard_map/ppermute | solution.py:45
  68.5 3.9 %collective-permute-start.4 = (f32[8,1,1024]{2,1,0:T(1,128)S(1)}, f32[8,1,1024]{2,1,0:T(1,128)S(1)}, u32[]{:S(2)}, u32[]{:S(2)}) collective-permute-start(f32[8,1,1024]{2,1,0:T(1,128)S(1)} %get-tuple-element.44), channel_id=1, source_target_pairs={{0,1},{1,2},{2,3},{3,4},{4,5},{5,6},{6,7},{7,8},{8,9},{9,10},{10,1... | collective-permute-start | bytes 98312 | tf_op jit(solution)/shard_map/ppermute | solution.py:43
  74.0 4.2 %collective-permute-done.5 = f32[8,1,1024]{2,1,0:T(1,128)S(1)} collective-permute-done((f32[8,1,1024]{2,1,0:T(1,128)S(1)}, f32[8,1,1024]{2,1,0:T(1,128)S(1)}, u32[]{:S(2)}, u32[]{:S(2)}) %collective-permute-start.5) | collective-permute-done | bytes 32800 | tf_op jit(solution)/shard_map/ppermute | solution.py:45
  79.1 2.2 %collective-permute-start.6 = (f32[8,1,1024]{2,1,0:T(1,128)S(1)}, f32[8,1,1024]{2,1,0:T(1,128)S(1)}, u32[]{:S(2)}, u32[]{:S(2)}) collective-permute-start(f32[8,1,1024]{2,1,0:T(1,128)S(1)} %get-tuple-element.42), channel_id=1, source_target_pairs={{0,1},{1,2},{2,3},{3,4},{4,5},{5,6},{6,7},{7,8},{8,9},{9,10},{10,1... | collective-permute-start | bytes 98312 | tf_op jit(solution)/shard_map/ppermute | solution.py:43
  83.0 4.2 %collective-permute-done.7 = f32[8,1,1024]{2,1,0:T(1,128)S(1)} collective-permute-done((f32[8,1,1024]{2,1,0:T(1,128)S(1)}, f32[8,1,1024]{2,1,0:T(1,128)S(1)}, u32[]{:S(2)}, u32[]{:S(2)}) %collective-permute-start.7) | collective-permute-done | bytes 32800 | tf_op jit(solution)/shard_map/ppermute | solution.py:45
  88.1 2.9 %collective-permute-start.8 = (f32[8,1,1024]{2,1,0:T(1,128)S(1)}, f32[8,1,1024]{2,1,0:T(1,128)S(1)}, u32[]{:S(2)}, u32[]{:S(2)}) collective-permute-start(f32[8,1,1024]{2,1,0:T(1,128)S(1)} %get-tuple-element.40), channel_id=1, source_target_pairs={{0,1},{1,2},{2,3},{3,4},{4,5},{5,6},{6,7},{7,8},{8,9},{9,10},{10,1... | collective-permute-start | bytes 98312 | tf_op jit(solution)/shard_map/ppermute | solution.py:43
  92.6 4.2 %collective-permute-done.9 = f32[8,1,1024]{2,1,0:T(1,128)S(1)} collective-permute-done((f32[8,1,1024]{2,1,0:T(1,128)S(1)}, f32[8,1,1024]{2,1,0:T(1,128)S(1)}, u32[]{:S(2)}, u32[]{:S(2)}) %collective-permute-start.9) | collective-permute-done | bytes 32800 | tf_op jit(solution)/shard_map/ppermute | solution.py:45
  97.7 4.1 %collective-permute-start.10 = (f32[8,1,1024]{2,1,0:T(1,128)S(1)}, f32[8,1,1024]{2,1,0:T(1,128)S(1)}, u32[]{:S(2)}, u32[]{:S(2)}) collective-permute-start(f32[8,1,1024]{2,1,0:T(1,128)S(1)} %get-tuple-element.38), channel_id=1, source_target_pairs={{0,1},{1,2},{2,3},{3,4},{4,5},{5,6},{6,7},{7,8},{8,9},{9,10},{10,1... | collective-permute-start | bytes 98312 | tf_op jit(solution)/shard_map/ppermute | solution.py:43
  103.4 4.6 %collective-permute-done.11 = f32[8,1,1024]{2,1,0:T(1,128)S(1)} collective-permute-done((f32[8,1,1024]{2,1,0:T(1,128)S(1)}, f32[8,1,1024]{2,1,0:T(1,128)S(1)}, u32[]{:S(2)}, u32[]{:S(2)}) %collective-permute-start.11) | collective-permute-done | bytes 32800 | tf_op jit(solution)/shard_map/ppermute | solution.py:45
  108.9 3.9 %collective-permute-start.12 = (f32[8,1,1024]{2,1,0:T(1,128)S(1)}, f32[8,1,1024]{2,1,0:T(1,128)S(1)}, u32[]{:S(2)}, u32[]{:S(2)}) collective-permute-start(f32[8,1,1024]{2,1,0:T(1,128)S(1)} %get-tuple-element.36), channel_id=1, source_target_pairs={{0,1},{1,2},{2,3},{3,4},{4,5},{5,6},{6,7},{7,8},{8,9},{9,10},{10,1... | collective-permute-start | bytes 98312 | tf_op jit(solution)/shard_map/ppermute | solution.py:43
  114.4 4.6 %collective-permute-done.13 = f32[8,1,1024]{2,1,0:T(1,128)S(1)} collective-permute-done((f32[8,1,1024]{2,1,0:T(1,128)S(1)}, f32[8,1,1024]{2,1,0:T(1,128)S(1)}, u32[]{:S(2)}, u32[]{:S(2)}) %collective-permute-start.13) | collective-permute-done | bytes 32800 | tf_op jit(solution)/shard_map/ppermute | solution.py:45
  119.8 3.7 %collective-permute-start.14 = (f32[8,1,1024]{2,1,0:T(1,128)S(1)}, f32[8,1,1024]{2,1,0:T(1,128)S(1)}, u32[]{:S(2)}, u32[]{:S(2)}) collective-permute-start(f32[8,1,1024]{2,1,0:T(1,128)S(1)} %get-tuple-element.34), channel_id=1, source_target_pairs={{0,1},{1,2},{2,3},{3,4},{4,5},{5,6},{6,7},{7,8},{8,9},{9,10},{10,1... | collective-permute-start | bytes 98312 | tf_op jit(solution)/shard_map/ppermute | solution.py:43
  123.5 1.5 collective-permute-start.15
  125.1 4.6 %collective-permute-done.15 = f32[8,1,1024]{2,1,0:T(1,128)S(1)} collective-permute-done((f32[8,1,1024]{2,1,0:T(1,128)S(1)}, f32[8,1,1024]{2,1,0:T(1,128)S(1)}, u32[]{:S(2)}, u32[]{:S(2)}) %collective-permute-start.15) | collective-permute-done | bytes 32800 | tf_op jit(solution)/shard_map/ppermute | solution.py:45
  130.6 3.7 %collective-permute-start.16 = (f32[8,1,1024]{2,1,0:T(1,128)S(1)}, f32[8,1,1024]{2,1,0:T(1,128)S(1)}, u32[]{:S(2)}, u32[]{:S(2)}) collective-permute-start(f32[8,1,1024]{2,1,0:T(1,128)S(1)} %get-tuple-element.32), channel_id=1, source_target_pairs={{0,1},{1,2},{2,3},{3,4},{4,5},{5,6},{6,7},{7,8},{8,9},{9,10},{10,1... | collective-permute-start | bytes 98312 | tf_op jit(solution)/shard_map/ppermute | solution.py:43
  135.9 4.6 %collective-permute-done.17 = f32[8,1,1024]{2,1,0:T(1,128)S(1)} collective-permute-done((f32[8,1,1024]{2,1,0:T(1,128)S(1)}, f32[8,1,1024]{2,1,0:T(1,128)S(1)}, u32[]{:S(2)}, u32[]{:S(2)}) %collective-permute-start.17) | collective-permute-done | bytes 32800 | tf_op jit(solution)/shard_map/ppermute | solution.py:45
  142.6 4.5 %collective-permute-start.26 = (f32[8,1,1024]{2,1,0:T(1,128)S(1)}, f32[8,1,1024]{2,1,0:T(1,128)S(1)}, u32[]{:S(2)}, u32[]{:S(2)}) collective-permute-start(f32[8,1,1024]{2,1,0:T(1,128)S(1)} %get-tuple-element.23), channel_id=1, source_target_pairs={{0,1},{1,2},{2,3},{3,4},{4,5},{5,6},{6,7},{7,8},{8,9},{9,10},{10,1... | collective-permute-start | bytes 98312 | tf_op jit(solution)/shard_map/ppermute | solution.py:43
  147.2 4.0 %collective-permute-start.18 = (f32[1,8,8,128]{3,2,1,0:T(8,128)S(1)}, f32[1,8,8,128]{3,2,1,0:T(8,128)S(1)}, u32[]{:S(2)}, u32[]{:S(2)}) collective-permute-start(f32[1,8,8,128]{3,2,1,0:T(8,128)S(1)} %get-tuple-element.31), channel_id=1, source_target_pairs={{0,4},{4,8},{8,12},{12,16},{16,20},{20,24},{24,28},{28,0},{1,5},{5... | collective-permute-start | bytes 98312 | tf_op jit(solution)/shard_map/ppermute | solution.py:30
  151.2 7.7 %collective-permute-start.19 = (f32[1,8,8,128]{3,2,1,0:T(8,128)S(1)}, f32[1,8,8,128]{3,2,1,0:T(8,128)S(1)}, u32[]{:S(2)}, u32[]{:S(2)}) collective-permute-start(f32[1,8,8,128]{3,2,1,0:T(8,128)S(1)} %get-tuple-element.30), channel_id=1, source_target_pairs={{0,8},{4,12},{8,16},{12,20},{16,24},{20,28},{24,0},{28,4},{1,9},{5... | collective-permute-start | bytes 98312 | tf_op jit(solution)/shard_map/ppermute | solution.py:30
  158.8 7.1 %collective-permute-start.20 = (f32[1,8,8,128]{3,2,1,0:T(8,128)S(1)}, f32[1,8,8,128]{3,2,1,0:T(8,128)S(1)}, u32[]{:S(2)}, u32[]{:S(2)}) collective-permute-start(f32[1,8,8,128]{3,2,1,0:T(8,128)S(1)} %get-tuple-element.29), channel_id=1, source_target_pairs={{0,12},{4,16},{8,20},{12,24},{16,28},{20,0},{24,4},{28,8},{1,13},{... | collective-permute-start | bytes 98312 | tf_op jit(solution)/shard_map/ppermute | solution.py:30
  168.0 1.9 collective-permute-start.23
  169.9 3.7 %collective-permute-start.24 = (f32[1,8,8,128]{3,2,1,0:T(8,128)S(1)}, f32[1,8,8,128]{3,2,1,0:T(8,128)S(1)}, u32[]{:S(2)}, u32[]{:S(2)}) collective-permute-start(f32[1,8,8,128]{3,2,1,0:T(8,128)S(1)} %get-tuple-element.25), channel_id=1, source_target_pairs={{0,28},{4,0},{8,4},{12,8},{16,12},{20,16},{24,20},{28,24},{1,29},{... | collective-permute-start | bytes 98312 | tf_op jit(solution)/shard_map/ppermute | solution.py:30
  173.7 1.5 collective-permute-done.24
  176.6 3.4 %all-to-all-start.2 = ((f32[1,8,64,128]{3,1,0,2:T(8,128)}), f32[1,8,64,128]{3,1,0,2:T(8,128)S(1)}, u32[]{:S(2)}, u32[]{:S(2)}) async-start(f32[1,8,64,128]{3,1,0,2:T(8,128)} %copy.30), calls=%async_computation.2 | async-start | bytes 524288 | tf_op jit(solution)/shard_map/all_to_all | solution.py:147
  181.5 7.1 %all-to-all-done.2 = f32[1,8,64,128]{3,1,0,2:T(8,128)S(1)} async-done(((f32[1,8,64,128]{3,1,0,2:T(8,128)}), f32[1,8,64,128]{3,1,0,2:T(8,128)S(1)}, u32[]{:S(2)}, u32[]{:S(2)}) %all-to-all-start.2) | async-done | bytes 262176 | tf_op jit(solution)/shard_map/all_to_all | solution.py:147
  (91 shorter events, 32.4 us)
Async XLA Ops:
  1.8 30.6 %copy-start = (f32[8,8,1024]{2,1,0:T(8,128)S(1)}, f32[8,8,1024]{2,1,0:T(8,128)}, u32[]{:S(2)}) copy-start(f32[8,8,1024]{2,1,0:T(8,128)} %param.5) | copy-start | bytes 786436
  1.8 30.6 %copy-start.2 = (s32[8,8,1024]{2,1,0:T(8,128)S(1)}, s32[8,8,1024]{2,1,0:T(8,128)}, u32[]{:S(2)}) copy-start(s32[8,8,1024]{2,1,0:T(8,128)} %param.4) | copy-start | bytes 786436
  28.7 16.3 %all-to-all-start.1 = ((f32[3,8,64,128]{3,1,0,2:T(8,128)}), f32[3,8,64,128]{3,1,0,2:T(8,128)S(1)}, u32[]{:S(2)}, u32[]{:S(2)}) async-start(f32[3,8,64,128]{3,1,0,2:T(8,128)} %all_to_all.28), calls=%async_computation.1 | async-start | bytes 1572864 | tf_op jit(solution)/shard_map/all_to_all | solution.py:155
  45.3 4.6 %collective-permute-start = (f32[4,8,1,1024]{3,2,1,0:T(1,128)S(1)}, f32[4,8,1,1024]{3,2,1,0:T(1,128)S(1)}, u32[]{:S(2)}, u32[]{:S(2)}) collective-permute-start(f32[4,8,1,1024]{3,2,1,0:T(1,128)S(1)} %get-tuple-element.9), channel_id=1, source_target_pairs={{0,1},{1,2},{2,3},{3,4},{4,5},{5,6},{6,7},{7,8},{8,9},{9,10},{10,1... | collective-permute-start | bytes 393224 | tf_op jit(solution)/shard_map/ppermute | solution.py:43
  47.4 7.3 %collective-permute-start.1 = (f32[4,8,1,1024]{3,2,1,0:T(1,128)S(1)}, f32[4,8,1,1024]{3,2,1,0:T(1,128)S(1)}, u32[]{:S(2)}, u32[]{:S(2)}) collective-permute-start(f32[4,8,1,1024]{3,2,1,0:T(1,128)S(1)} %get-tuple-element.10), channel_id=1, source_target_pairs={{1,0},{2,1},{3,2},{4,3},{5,4},{6,5},{7,6},{8,7},{9,8},{10,9},{11,1... | collective-permute-start | bytes 393224 | tf_op jit(solution)/shard_map/ppermute | solution.py:45
  56.4 1.1 copy-start.1
  58.9 4.2 %collective-permute-start.2 = (f32[1,8,1,1024]{3,2,1,0:T(1,128)S(1)}, f32[1,8,1,1024]{3,2,1,0:T(1,128)S(1)}, u32[]{:S(2)}, u32[]{:S(2)}) collective-permute-start(f32[1,8,1,1024]{3,2,1,0:T(1,128)S(1)} %get-tuple-element.11), channel_id=1, source_target_pairs={{0,1},{1,2},{2,3},{3,4},{4,5},{5,6},{6,7},{7,8},{8,9},{9,10},{10,1... | collective-permute-start | bytes 98312 | tf_op jit(solution)/shard_map/ppermute | solution.py:43
  61.4 6.3 %collective-permute-start.3 = (f32[1,8,1,1024]{3,2,1,0:T(1,128)S(1)}, f32[1,8,1,1024]{3,2,1,0:T(1,128)S(1)}, u32[]{:S(2)}, u32[]{:S(2)}) collective-permute-start(f32[1,8,1,1024]{3,2,1,0:T(1,128)S(1)} %get-tuple-element.12), channel_id=1, source_target_pairs={{1,0},{2,1},{3,2},{4,3},{5,4},{6,5},{7,6},{8,7},{9,8},{10,9},{11,1... | collective-permute-start | bytes 98312 | tf_op jit(solution)/shard_map/ppermute | solution.py:45
  68.5 5.5 %collective-permute-start.4 = (f32[8,1,1024]{2,1,0:T(1,128)S(1)}, f32[8,1,1024]{2,1,0:T(1,128)S(1)}, u32[]{:S(2)}, u32[]{:S(2)}) collective-permute-start(f32[8,1,1024]{2,1,0:T(1,128)S(1)} %get-tuple-element.44), channel_id=1, source_target_pairs={{0,1},{1,2},{2,3},{3,4},{4,5},{5,6},{6,7},{7,8},{8,9},{9,10},{10,1... | collective-permute-start | bytes 98312 | tf_op jit(solution)/shard_map/ppermute | solution.py:43
  72.5 5.8 %collective-permute-start.5 = (f32[8,1,1024]{2,1,0:T(1,128)S(1)}, f32[8,1,1024]{2,1,0:T(1,128)S(1)}, u32[]{:S(2)}, u32[]{:S(2)}) collective-permute-start(f32[8,1,1024]{2,1,0:T(1,128)S(1)} %get-tuple-element.45), channel_id=1, source_target_pairs={{1,0},{2,1},{3,2},{4,3},{5,4},{6,5},{7,6},{8,7},{9,8},{10,9},{11,1... | collective-permute-start | bytes 98312 | tf_op jit(solution)/shard_map/ppermute | solution.py:45
  79.1 3.8 %collective-permute-start.6 = (f32[8,1,1024]{2,1,0:T(1,128)S(1)}, f32[8,1,1024]{2,1,0:T(1,128)S(1)}, u32[]{:S(2)}, u32[]{:S(2)}) collective-permute-start(f32[8,1,1024]{2,1,0:T(1,128)S(1)} %get-tuple-element.42), channel_id=1, source_target_pairs={{0,1},{1,2},{2,3},{3,4},{4,5},{5,6},{6,7},{7,8},{8,9},{9,10},{10,1... | collective-permute-start | bytes 98312 | tf_op jit(solution)/shard_map/ppermute | solution.py:43
  81.4 5.8 %collective-permute-start.7 = (f32[8,1,1024]{2,1,0:T(1,128)S(1)}, f32[8,1,1024]{2,1,0:T(1,128)S(1)}, u32[]{:S(2)}, u32[]{:S(2)}) collective-permute-start(f32[8,1,1024]{2,1,0:T(1,128)S(1)} %get-tuple-element.43), channel_id=1, source_target_pairs={{1,0},{2,1},{3,2},{4,3},{5,4},{6,5},{7,6},{8,7},{9,8},{10,9},{11,1... | collective-permute-start | bytes 98312 | tf_op jit(solution)/shard_map/ppermute | solution.py:45
  88.1 4.5 %collective-permute-start.8 = (f32[8,1,1024]{2,1,0:T(1,128)S(1)}, f32[8,1,1024]{2,1,0:T(1,128)S(1)}, u32[]{:S(2)}, u32[]{:S(2)}) collective-permute-start(f32[8,1,1024]{2,1,0:T(1,128)S(1)} %get-tuple-element.40), channel_id=1, source_target_pairs={{0,1},{1,2},{2,3},{3,4},{4,5},{5,6},{6,7},{7,8},{8,9},{9,10},{10,1... | collective-permute-start | bytes 98312 | tf_op jit(solution)/shard_map/ppermute | solution.py:43
  91.0 5.8 %collective-permute-start.9 = (f32[8,1,1024]{2,1,0:T(1,128)S(1)}, f32[8,1,1024]{2,1,0:T(1,128)S(1)}, u32[]{:S(2)}, u32[]{:S(2)}) collective-permute-start(f32[8,1,1024]{2,1,0:T(1,128)S(1)} %get-tuple-element.41), channel_id=1, source_target_pairs={{1,0},{2,1},{3,2},{4,3},{5,4},{6,5},{7,6},{8,7},{9,8},{10,9},{11,1... | collective-permute-start | bytes 98312 | tf_op jit(solution)/shard_map/ppermute | solution.py:45
  97.7 5.7 %collective-permute-start.10 = (f32[8,1,1024]{2,1,0:T(1,128)S(1)}, f32[8,1,1024]{2,1,0:T(1,128)S(1)}, u32[]{:S(2)}, u32[]{:S(2)}) collective-permute-start(f32[8,1,1024]{2,1,0:T(1,128)S(1)} %get-tuple-element.38), channel_id=1, source_target_pairs={{0,1},{1,2},{2,3},{3,4},{4,5},{5,6},{6,7},{7,8},{8,9},{9,10},{10,1... | collective-permute-start | bytes 98312 | tf_op jit(solution)/shard_map/ppermute | solution.py:43
  101.8 6.2 %collective-permute-start.11 = (f32[8,1,1024]{2,1,0:T(1,128)S(1)}, f32[8,1,1024]{2,1,0:T(1,128)S(1)}, u32[]{:S(2)}, u32[]{:S(2)}) collective-permute-start(f32[8,1,1024]{2,1,0:T(1,128)S(1)} %get-tuple-element.39), channel_id=1, source_target_pairs={{1,0},{2,1},{3,2},{4,3},{5,4},{6,5},{7,6},{8,7},{9,8},{10,9},{11,1... | collective-permute-start | bytes 98312 | tf_op jit(solution)/shard_map/ppermute | solution.py:45
  108.9 5.5 %collective-permute-start.12 = (f32[8,1,1024]{2,1,0:T(1,128)S(1)}, f32[8,1,1024]{2,1,0:T(1,128)S(1)}, u32[]{:S(2)}, u32[]{:S(2)}) collective-permute-start(f32[8,1,1024]{2,1,0:T(1,128)S(1)} %get-tuple-element.36), channel_id=1, source_target_pairs={{0,1},{1,2},{2,3},{3,4},{4,5},{5,6},{6,7},{7,8},{8,9},{9,10},{10,1... | collective-permute-start | bytes 98312 | tf_op jit(solution)/shard_map/ppermute | solution.py:43
  112.8 6.1 %collective-permute-start.13 = (f32[8,1,1024]{2,1,0:T(1,128)S(1)}, f32[8,1,1024]{2,1,0:T(1,128)S(1)}, u32[]{:S(2)}, u32[]{:S(2)}) collective-permute-start(f32[8,1,1024]{2,1,0:T(1,128)S(1)} %get-tuple-element.37), channel_id=1, source_target_pairs={{1,0},{2,1},{3,2},{4,3},{5,4},{6,5},{7,6},{8,7},{9,8},{10,9},{11,1... | collective-permute-start | bytes 98312 | tf_op jit(solution)/shard_map/ppermute | solution.py:45
  119.8 5.3 %collective-permute-start.14 = (f32[8,1,1024]{2,1,0:T(1,128)S(1)}, f32[8,1,1024]{2,1,0:T(1,128)S(1)}, u32[]{:S(2)}, u32[]{:S(2)}) collective-permute-start(f32[8,1,1024]{2,1,0:T(1,128)S(1)} %get-tuple-element.34), channel_id=1, source_target_pairs={{0,1},{1,2},{2,3},{3,4},{4,5},{5,6},{6,7},{7,8},{8,9},{9,10},{10,1... | collective-permute-start | bytes 98312 | tf_op jit(solution)/shard_map/ppermute | solution.py:43
  123.5 6.1 %collective-permute-start.15 = (f32[8,1,1024]{2,1,0:T(1,128)S(1)}, f32[8,1,1024]{2,1,0:T(1,128)S(1)}, u32[]{:S(2)}, u32[]{:S(2)}) collective-permute-start(f32[8,1,1024]{2,1,0:T(1,128)S(1)} %get-tuple-element.35), channel_id=1, source_target_pairs={{1,0},{2,1},{3,2},{4,3},{5,4},{6,5},{7,6},{8,7},{9,8},{10,9},{11,1... | collective-permute-start | bytes 98312 | tf_op jit(solution)/shard_map/ppermute | solution.py:45
  130.6 5.3 %collective-permute-start.16 = (f32[8,1,1024]{2,1,0:T(1,128)S(1)}, f32[8,1,1024]{2,1,0:T(1,128)S(1)}, u32[]{:S(2)}, u32[]{:S(2)}) collective-permute-start(f32[8,1,1024]{2,1,0:T(1,128)S(1)} %get-tuple-element.32), channel_id=1, source_target_pairs={{0,1},{1,2},{2,3},{3,4},{4,5},{5,6},{6,7},{7,8},{8,9},{9,10},{10,1... | collective-permute-start | bytes 98312 | tf_op jit(solution)/shard_map/ppermute | solution.py:43
  134.3 6.1 %collective-permute-start.17 = (f32[8,1,1024]{2,1,0:T(1,128)S(1)}, f32[8,1,1024]{2,1,0:T(1,128)S(1)}, u32[]{:S(2)}, u32[]{:S(2)}) collective-permute-start(f32[8,1,1024]{2,1,0:T(1,128)S(1)} %get-tuple-element.33), channel_id=1, source_target_pairs={{1,0},{2,1},{3,2},{4,3},{5,4},{6,5},{7,6},{8,7},{9,8},{10,9},{11,1... | collective-permute-start | bytes 98312 | tf_op jit(solution)/shard_map/ppermute | solution.py:45
  141.3 24.6 %collective-permute-start.25 = (f32[8,1,1024]{2,1,0:T(1,128)S(1)}, f32[8,1,1024]{2,1,0:T(1,128)S(1)}, u32[]{:S(2)}, u32[]{:S(2)}) collective-permute-start(f32[8,1,1024]{2,1,0:T(1,128)S(1)} %get-tuple-element.24), channel_id=1, source_target_pairs={{1,0},{2,1},{3,2},{4,3},{5,4},{6,5},{7,6},{8,7},{9,8},{10,9},{11,1... | collective-permute-start | bytes 98312 | tf_op jit(solution)/shard_map/ppermute | solution.py:45
  142.6 23.3 %collective-permute-start.26 = (f32[8,1,1024]{2,1,0:T(1,128)S(1)}, f32[8,1,1024]{2,1,0:T(1,128)S(1)}, u32[]{:S(2)}, u32[]{:S(2)}) collective-permute-start(f32[8,1,1024]{2,1,0:T(1,128)S(1)} %get-tuple-element.23), channel_id=1, source_target_pairs={{0,1},{1,2},{2,3},{3,4},{4,5},{5,6},{6,7},{7,8},{8,9},{9,10},{10,1... | collective-permute-start | bytes 98312 | tf_op jit(solution)/shard_map/ppermute | solution.py:43
  147.2 20.8 %collective-permute-start.18 = (f32[1,8,8,128]{3,2,1,0:T(8,128)S(1)}, f32[1,8,8,128]{3,2,1,0:T(8,128)S(1)}, u32[]{:S(2)}, u32[]{:S(2)}) collective-permute-start(f32[1,8,8,128]{3,2,1,0:T(8,128)S(1)} %get-tuple-element.31), channel_id=1, source_target_pairs={{0,4},{4,8},{8,12},{12,16},{16,20},{20,24},{24,28},{28,0},{1,5},{5... | collective-permute-start | bytes 98312 | tf_op jit(solution)/shard_map/ppermute | solution.py:30
  151.2 18.7 %collective-permute-start.19 = (f32[1,8,8,128]{3,2,1,0:T(8,128)S(1)}, f32[1,8,8,128]{3,2,1,0:T(8,128)S(1)}, u32[]{:S(2)}, u32[]{:S(2)}) collective-permute-start(f32[1,8,8,128]{3,2,1,0:T(8,128)S(1)} %get-tuple-element.30), channel_id=1, source_target_pairs={{0,8},{4,12},{8,16},{12,20},{16,24},{20,28},{24,0},{28,4},{1,9},{5... | collective-permute-start | bytes 98312 | tf_op jit(solution)/shard_map/ppermute | solution.py:30
  158.8 14.8 %collective-permute-start.20 = (f32[1,8,8,128]{3,2,1,0:T(8,128)S(1)}, f32[1,8,8,128]{3,2,1,0:T(8,128)S(1)}, u32[]{:S(2)}, u32[]{:S(2)}) collective-permute-start(f32[1,8,8,128]{3,2,1,0:T(8,128)S(1)} %get-tuple-element.29), channel_id=1, source_target_pairs={{0,12},{4,16},{8,20},{12,24},{16,28},{20,0},{24,4},{28,8},{1,13},{... | collective-permute-start | bytes 98312 | tf_op jit(solution)/shard_map/ppermute | solution.py:30
  165.9 7.7 %collective-permute-start.21 = (f32[1,8,8,128]{3,2,1,0:T(8,128)S(1)}, f32[1,8,8,128]{3,2,1,0:T(8,128)S(1)}, u32[]{:S(2)}, u32[]{:S(2)}) collective-permute-start(f32[1,8,8,128]{3,2,1,0:T(8,128)S(1)} %get-tuple-element.28), channel_id=1, source_target_pairs={{0,16},{4,20},{8,24},{12,28},{16,0},{20,4},{24,8},{28,12},{1,17},{... | collective-permute-start | bytes 98312 | tf_op jit(solution)/shard_map/ppermute | solution.py:30
  165.9 7.7 %collective-permute-start.22 = (f32[1,8,8,128]{3,2,1,0:T(8,128)S(1)}, f32[1,8,8,128]{3,2,1,0:T(8,128)S(1)}, u32[]{:S(2)}, u32[]{:S(2)}) collective-permute-start(f32[1,8,8,128]{3,2,1,0:T(8,128)S(1)} %get-tuple-element.27), channel_id=1, source_target_pairs={{0,20},{4,24},{8,28},{12,0},{16,4},{20,8},{24,12},{28,16},{1,21},{... | collective-permute-start | bytes 98312 | tf_op jit(solution)/shard_map/ppermute | solution.py:30
  168.0 5.6 %collective-permute-start.23 = (f32[1,8,8,128]{3,2,1,0:T(8,128)S(1)}, f32[1,8,8,128]{3,2,1,0:T(8,128)S(1)}, u32[]{:S(2)}, u32[]{:S(2)}) collective-permute-start(f32[1,8,8,128]{3,2,1,0:T(8,128)S(1)} %get-tuple-element.26), channel_id=1, source_target_pairs={{0,24},{4,28},{8,0},{12,4},{16,8},{20,12},{24,16},{28,20},{1,25},{... | collective-permute-start | bytes 98312 | tf_op jit(solution)/shard_map/ppermute | solution.py:30
  169.9 5.3 %collective-permute-start.24 = (f32[1,8,8,128]{3,2,1,0:T(8,128)S(1)}, f32[1,8,8,128]{3,2,1,0:T(8,128)S(1)}, u32[]{:S(2)}, u32[]{:S(2)}) collective-permute-start(f32[1,8,8,128]{3,2,1,0:T(8,128)S(1)} %get-tuple-element.25), channel_id=1, source_target_pairs={{0,28},{4,0},{8,4},{12,8},{16,12},{20,16},{24,20},{28,24},{1,29},{... | collective-permute-start | bytes 98312 | tf_op jit(solution)/shard_map/ppermute | solution.py:30
  176.6 11.9 %all-to-all-start.2 = ((f32[1,8,64,128]{3,1,0,2:T(8,128)}), f32[1,8,64,128]{3,1,0,2:T(8,128)S(1)}, u32[]{:S(2)}, u32[]{:S(2)}) async-start(f32[1,8,64,128]{3,1,0,2:T(8,128)} %copy.30), calls=%async_computation.2 | async-start | bytes 524288 | tf_op jit(solution)/shard_map/all_to_all | solution.py:147
